TPU v7x, 32 devices: a whole 2x2x4 slice. The times are simulated.
32 devices in a mesh: grp: 4 (over y, core), span: 8 (over z, x).
Axes of the slice: x: 2, y: 2, z: 4, core: 2. Of those that a mesh axis runs over, the one named last changes fastest.
Arguments:
- record: float32 [131072, 128], P(('grp', 'span')), may hold values from -96 to 96, as said below
Outputs:
- triangle: float32 [512, 512], replicated
- operator: float32 [512, 512], replicated
Inputs may be any that keep to these rules, and one draw needn't show every extreme that they name: `record`: Real-valued probe samples.
All inputs are finite; a program needn't handle non-finite values.
Results may differ from a plain program's by a relative error of at most 0.0003.
Values sent between devices are 32-bit elements; how exact they have to be, the bound alone decides.
A program may use at most 64 MiB of HBM per device.

v0:
```python
import jax
import jax.numpy as jnp
from jax import lax
from jax.sharding import PartitionSpec as P

LAGS = 4
DELAY = 1024


def shifted(value, axis, steps):
    count = lax.axis_size(axis)
    leading, last = (max(0, -steps), min(count, count - steps))
    return lax.ppermute(value, axis, [(source, source + steps) for source in range(leading, last)])


def inner_rows(left, right):
    return lax.dot_general(
        left,
        right,
        (((0,), (0,)), ((), ())),
        precision=lax.Precision.HIGHEST,
        preferred_element_type=jnp.float32,
    )


def on_device(record):
    count = record.shape[0]
    lead = (LAGS - 1) * DELAY + 1
    following = shifted(record[:lead], ("grp", "span"), -1)
    ext = jnp.concatenate([record, following], 0)
    hank = jnp.concatenate([ext[k * DELAY : k * DELAY + count + 1] for k in range(LAGS)], 1)
    devices = lax.axis_size(("grp", "span"))
    last_row = count * devices - lead
    times = lax.axis_index(("grp", "span")) * count + jnp.arange(count, dtype=jnp.int32)
    weight = (
        jnp.where(times < last_row, 1.0, 0.0)
        - 0.5 * jnp.where(times == 0, 1.0, 0.0)
        - 0.5 * jnp.where(times == last_row, 1.0, 0.0)
    )
    weight = weight.astype(jnp.float32)
    inside = jnp.where(times < last_row, 1.0, 0.0).astype(jnp.float32)
    head = hank[:count]
    weighted = head * weight[:, None]
    cross = inner_rows(head * inside[:, None], hank[1 : count + 1])
    scale = 1.0 / last_row
    gram = inner_rows(weighted, head)
    gram, cross = lax.psum((gram, cross), ("grp", "span"))
    lower = jnp.linalg.cholesky(gram * scale)
    middle = jax.scipy.linalg.solve_triangular(lower, cross * scale, lower=True)
    operator = jax.scipy.linalg.solve_triangular(lower, middle.T, lower=True).T
    return (lower.T, operator)


def solution(mesh):
    placed = (P(("grp", "span"), None),)
    return jax.shard_map(
        on_device, mesh=mesh, in_specs=placed, out_specs=(P(), P()), check_vma=False
    )
```

profile of v0, /device:TPU:0, one launch (start us, length us, event | category | flops | bytes accessed | tf_op | source)
XLA Modules:
  0.0 379.2 jit_solution(13203362706034608490)
XLA Ops:
  7.2 1.5 slice.124
  8.7 1.3 collective-permute-start
  10.0 1.7 constant_dynamic-update-slice_fusion.1
  11.8 36.3 %collective-permute-done = f32[3073,128]{1,0:T(8,128)S(1)} collective-permute-done((f32[3073,128]{1,0:T(8,128)S(1)}, f32[3073,128]{1,0:T(8,128)S(1)}, u32[]{:S(2)}, u32[]{:S(2)}) %collective-permute-start) | collective-permute-done | bytes 1573408 | tf_op jit(solution)/shard_map/ppermute | solution.py:13
  48.1 0.1 constant_dynamic-update-slice_fusion
  48.2 0.5 fusion.64
  48.7 1.4 pad_maximum_fusion
  50.1 17.3 %fusion.2 = f32[512,512]{0,1:T(8,128)} fusion(f32[4097,512]{1,0:T(8,128)S(1)} %pad_maximum_fusion, f32[4096]{0:T(1024)S(1)} %get-tuple-element.52), kind=kOutput, calls=%fused_computation.5 | convolution fusion | flops 12886999040 | bytes 17842176 | tf_op jit(solution)/shard_map/dot_general | solution.py:17
  67.4 16.4 %fusion = f32[512,512]{0,1:T(8,128)} fusion(f32[4097,512]{1,0:T(8,128)S(1)} %pad_maximum_fusion, f32[4096]{0:T(1024)S(1)} %get-tuple-element.51), kind=kOutput, calls=%fused_computation.2 | convolution fusion | flops 12886999040 | bytes 17842176 | tf_op jit(solution)/shard_map/dot_general | solution.py:17
  83.8 139.5 %all-reduce.4.cloned.1.call-done = (f32[512,512]{0,1:T(8,128)}, f32[512,512]{0,1:T(8,128)}) async-done(((f32[512,512]{0,1:T(8,128)}, f32[512,512]{0,1:T(8,128)}), (f32[512,512]{0,1:T(8,128)}, f32[512,512]{0,1:T(8,128)})) %all-reduce.4.cloned.1.call-update) | async-done | bytes 2097168 | tf_op jit(solution)/shard_map/psum | solution.py:47
  223.3 1.3 broadcast_multiply_fusion.1
  224.6 0.3 copy.4
  225.0 1.5 fusion.9
  226.5 11.7 %cholesky.104 = f32[128,128]{1,0:T(8,128)S(1)} custom-call(f32[128,128]{1,0:T(8,128)S(1)} %cholesky.266), custom_call_target="Cholesky" | custom-call | tf_op jit(solution)/shard_map/jit(cholesky)/cholesky | solution.py:48
  238.2 9.8 %custom-call.30 = f32[1,128,128]{1,2,0:T(8,128)S(1)} custom-call(f32[1,128,128]{2,1,0:T(8,128)S(1)} %get-tuple-element.48), custom_call_target="InvertDiagBlocksLowerTriangular" | custom-call | tf_op jit(solution)/shard_map/jit(cholesky)/cholesky | solution.py:48
  248.0 0.1 cholesky.224
  248.1 0.3 constant_dynamic-update-slice_fusion.5
  248.5 0.3 convolution_subtract_fusion.6
  248.8 12.2 %cholesky.217 = f32[128,128]{1,0:T(8,128)S(1)} custom-call(f32[128,128]{1,0:T(8,128)S(1)} %cholesky.270), custom_call_target="Cholesky" | custom-call | tf_op jit(solution)/shard_map/jit(cholesky)/cholesky | solution.py:48
  261.0 0.6 compare_reduce_fusion.2
  261.7 0.6 compare_reduce_fusion.3
  262.3 9.8 %custom-call.31 = f32[1,128,128]{1,2,0:T(8,128)S(1)} custom-call(f32[1,128,128]{2,1,0:T(8,128)S(1)} %get-tuple-element.45), custom_call_target="InvertDiagBlocksLowerTriangular" | custom-call | tf_op jit(solution)/shard_map/jit(cholesky)/cholesky | solution.py:48
  272.1 0.3 convolution_dynamic-update-slice_fusion
  272.4 0.4 convolution_subtract_fusion.7
  272.8 11.7 %cholesky.238 = f32[128,128]{1,0:T(8,128)S(1)} custom-call(f32[128,128]{1,0:T(8,128)S(1)} %cholesky.275), custom_call_target="Cholesky" | custom-call | tf_op jit(solution)/shard_map/jit(cholesky)/cholesky | solution.py:48
  284.5 0.7 compare_reduce_fusion.1
  285.2 9.8 %custom-call.32 = f32[1,128,128]{1,2,0:T(8,128)S(1)} custom-call(f32[1,128,128]{2,1,0:T(8,128)S(1)} %get-tuple-element.42), custom_call_target="InvertDiagBlocksLowerTriangular" | custom-call | tf_op jit(solution)/shard_map/jit(cholesky)/cholesky | solution.py:48
  295.1 0.2 convolution_dynamic-update-slice_fusion.1
  295.3 0.4 convolution_subtract_fusion.8
  295.7 11.9 %cholesky.255 = f32[128,128]{1,0:T(8,128)S(1)} custom-call(f32[128,128]{1,0:T(8,128)S(1)} %convolution_subtract_fusion.8), custom_call_target="Cholesky" | custom-call | tf_op jit(solution)/shard_map/jit(cholesky)/cholesky | solution.py:48
  307.6 0.6 compare_reduce_fusion
  310.8 0.3 fusion.10
  311.0 8.0 %while.4 = (s32[]{:T(128)}, f32[512,512]{1,0:T(8,128)S(1)}, s32[4,2]{0,1:T(2,128)S(1)}, f32[4,128,128]{2,1,0:T(8,128)S(1)}, s32[]{:T(128)}) while((s32[]{:T(128)}, f32[512,512]{1,0:T(8,128)S(1)}, s32[4,2]{0,1:T(2,128)S(1)}, f32[4,128,128]{2,1,0:T(8,128)S(1)}, s32[]{:T(128)}) %tuple.41), condition=%wide.while_cond.clone, body=%wide.while_body.clone.sunk | while | flops 2 | bytes 131181 | solution.py:50
  311.0 0.1 constant_dynamic-slice_fusion.2
  311.1 0.5 fusion.75
  311.6 1.4 bitcast_dynamic-update-slice_fusion.2
  313.0 0.1 constant_dynamic-slice_fusion.2
  313.1 0.5 fusion.75
  313.6 1.4 bitcast_dynamic-update-slice_fusion.2
  315.0 0.1 constant_dynamic-slice_fusion.2
  315.1 0.5 fusion.75
  315.6 1.4 bitcast_dynamic-update-slice_fusion.2
  317.1 0.1 constant_dynamic-slice_fusion.2
  317.1 0.5 fusion.75
  317.6 1.4 bitcast_dynamic-update-slice_fusion.2
  319.0 39.3 %custom-call.35 = f32[4,128,128]{1,2,0:T(8,128)S(1)} custom-call(f32[4,128,128]{2,1,0:T(8,128)S(1)} %get-tuple-element.18), custom_call_target="InvertDiagBlocksLowerTriangular" | custom-call | tf_op jit(solution)/shard_map/jit(_solve_triangular)/triangular_solve | solution.py:50
  358.4 1.3 broadcast_multiply_fusion
  359.7 0.4 fusion.30
  360.2 0.6 convolution_subtract_fusion.3
  360.8 0.4 fusion.48
  361.2 1.0 convolution_subtract_fusion.2
  362.2 0.4 fusion.50
  362.6 1.5 convolution_subtract_fusion.5
  364.1 0.4 fusion.52
  364.5 0.1 maximum_bitcast_fusion
  364.6 0.4 fusion.28
  365.1 0.6 convolution_subtract_fusion.1
  365.7 0.4 fusion.47
  366.1 1.0 convolution_subtract_fusion
  367.1 0.4 fusion.49
  367.5 1.5 convolution_subtract_fusion.4
  369.0 0.4 fusion.51
  369.5 1.3 copy.7
  370.8 1.3 copy.6
  (14 shorter events, 0.3 us)
Async XLA Ops:
  7.2 216.1 %all-reduce.4.cloned.1.call-start = ((), (), s32[]{:S(2)}) async-start(), calls=%async_computation | async-start | bytes 4194304 | tf_op jit(solution)/shard_map/psum | solution.py:47
  8.7 39.3 %collective-permute-start = (f32[3073,128]{1,0:T(8,128)S(1)}, f32[3073,128]{1,0:T(8,128)S(1)}, u32[]{:S(2)}, u32[]{:S(2)}) collective-permute-start(f32[3073,128]{1,0:T(8,128)S(1)} %slice.124), channel_id=1, source_target_pairs={{1,0},{2,1},{3,2},{4,3},{5,4},{6,5},{7,6},{8,7},{9,8},{10,9},{11,1... | collective-permute-start | bytes 4720136 | tf_op jit(solution)/shard_map/ppermute | solution.py:13
Sparse Core Ops, SparseCore 0:
  83.9 139.3 all-reduce.3
where the time goes:
time: 384 us; the launch traced here: 379 us
  waiting for transfers between devices  176 us (46%)
  other arithmetic  125 us (33%)
  matrix products  45 us (12%)
  between operations  17.1 us (4%)
  local copies, waits for them, and re-layouts  14.9 us (4%)
    psum x1, waiting for transfers between devices, on_device(): gram, cross = lax.psum((gram, cross), ('grp', 'span'))  140 us
    another operation x15, other arithmetic, on_device(): lower = jnp.linalg.cholesky(gram * scale)  79.7 us
    another operation x4, other arithmetic, on_device(): operator = jax.scipy.linalg.solve_triangular(lower, middle.T, lower=True).T  39.6 us
    ppermute x1, waiting for transfers between devices, shifted(): lax.ppermute(value, axis, [(source, source + steps) for source in range(l...  36.3 us
    dot_general x2, matrix products, inner_rows(): lax.dot_general(left, right, (((0,), (0,)), ((), ())), precision=lax.Prec...  33.6 us
    another operation x13, local copies, waits for them, and re-layouts, on_device(): operator = jax.scipy.linalg.solve_triangular(lower, middle.T, lower=True).T  7.92 us
  transfers between devices with their start and end apart: 2, of which 2 were waited for; matrix products, arithmetic and copies ran while one was open for 0% of the time, Pallas kernels for 0%

commit v1 on v0

--- a/solution.py
+++ b/solution.py
@@ -5,6 +5,11 @@
 
 LAGS = 4
 DELAY = 1024
+
+
+def axis_by_axis(array, inner_axis, outer_axis):
+    partial = lax.psum(array, inner_axis)
+    return lax.psum(partial, outer_axis)
 
 
 def shifted(value, axis, steps):
@@ -44,7 +49,7 @@
     cross = inner_rows(head * inside[:, None], hank[1 : count + 1])
     scale = 1.0 / last_row
     gram = inner_rows(weighted, head)
-    gram, cross = lax.psum((gram, cross), ("grp", "span"))
+    gram, cross = axis_by_axis((gram, cross), "span", "grp")
     lower = jnp.linalg.cholesky(gram * scale)
     middle = jax.scipy.linalg.solve_triangular(lower, cross * scale, lower=True)
     operator = jax.scipy.linalg.solve_triangular(lower, middle.T, lower=True).T

time: 384 us -> 405 us (1.055)
  waiting for transfers between devices: 176 us -> 197 us
    psum x1 -> x2, waiting for transfers between devices: 140 us -> 160 us  [the longest x1 107 us: axis_by_axis(): partial = lax.psum(array, inner_axis)]
  transfers between devices with their start and end apart: 2 -> 3, of which waited for: 2 -> 3; matrix products, arithmetic and copies ran while one was open for 0% -> 0% of each run, Pallas kernels for 0% -> 0%
where the time goes in v1:
time: 405 us; the launch traced here: 400 us
  waiting for transfers between devices  197 us (49%)
  other arithmetic  125 us (31%)
  matrix products  45.2 us (11%)
  between operations  17.2 us (4%)
  local copies, waits for them, and re-layouts  14.9 us (4%)
    psum x1, waiting for transfers between devices, axis_by_axis(): partial = lax.psum(array, inner_axis)  107 us
    another operation x15, other arithmetic, on_device(): lower = jnp.linalg.cholesky(gram * scale)  79.4 us
    psum x1, waiting for transfers between devices, axis_by_axis(): return lax.psum(partial, outer_axis)  53.1 us
    another operation x4, other arithmetic, on_device(): operator = jax.scipy.linalg.solve_triangular(lower, middle.T, lower=True).T  39.6 us
    ppermute x1, waiting for transfers between devices, shifted(): lax.ppermute(value, axis, [(source, source + steps) for source in range(l...  36.3 us
    dot_general x2, matrix products, inner_rows(): lax.dot_general(left, right, (((0,), (0,)), ((), ())), precision=lax.Prec...  33.8 us
  transfers between devices with their start and end apart: 3, of which 3 were waited for; matrix products, arithmetic and copies ran while one was open for 0% of the time, Pallas kernels for 0%

profile of v1, /device:TPU:0, one launch (start us, length us, event | category | flops | bytes accessed | tf_op | source)
XLA Modules:
  0.0 400.0 jit_solution(7018317131418238983)
XLA Ops:
  7.2 1.5 slice.124
  8.7 1.3 collective-permute-start
  10.0 1.7 constant_dynamic-update-slice_fusion.1
  11.8 36.3 %collective-permute-done = f32[3073,128]{1,0:T(8,128)S(1)} collective-permute-done((f32[3073,128]{1,0:T(8,128)S(1)}, f32[3073,128]{1,0:T(8,128)S(1)}, u32[]{:S(2)}, u32[]{:S(2)}) %collective-permute-start) | collective-permute-done | bytes 1573408 | tf_op jit(solution)/shard_map/ppermute | solution.py:18
  48.1 0.1 constant_dynamic-update-slice_fusion
  48.2 0.5 fusion.64
  48.7 1.4 pad_maximum_fusion
  50.1 17.3 %fusion.2 = f32[512,512]{0,1:T(8,128)} fusion(f32[4097,512]{1,0:T(8,128)S(1)} %pad_maximum_fusion, f32[4096]{0:T(1024)S(1)} %get-tuple-element.54), kind=kOutput, calls=%fused_computation.5 | convolution fusion | flops 12886999040 | bytes 17842176 | tf_op jit(solution)/shard_map/dot_general | solution.py:22
  67.4 16.5 %fusion = f32[512,512]{0,1:T(8,128)} fusion(f32[4097,512]{1,0:T(8,128)S(1)} %pad_maximum_fusion, f32[4096]{0:T(1024)S(1)} %get-tuple-element.53), kind=kOutput, calls=%fused_computation.2 | convolution fusion | flops 12886999040 | bytes 17842176 | tf_op jit(solution)/shard_map/dot_general | solution.py:22
  84.0 107.2 %all-reduce.6.cloned.1.call-done = (f32[512,512]{0,1:T(8,128)}, f32[512,512]{0,1:T(8,128)}) async-done(((f32[512,512]{0,1:T(8,128)}, f32[512,512]{0,1:T(8,128)}), (f32[512,512]{0,1:T(8,128)}, f32[512,512]{0,1:T(8,128)})) %all-reduce.6.cloned.1.call-update) | async-done | bytes 2097168 | tf_op jit(solution)/shard_map/psum | solution.py:11
  191.2 53.1 %all-reduce.8.cloned.1.call-done = (f32[512,512]{0,1:T(8,128)}, f32[512,512]{0,1:T(8,128)}) async-done(((f32[512,512]{0,1:T(8,128)}, f32[512,512]{0,1:T(8,128)}), (f32[512,512]{0,1:T(8,128)}, f32[512,512]{0,1:T(8,128)})) %all-reduce.8.cloned.1.call-update) | async-done | bytes 2097168 | tf_op jit(solution)/shard_map/psum | solution.py:12
  244.3 1.3 broadcast_multiply_fusion.1
  245.7 0.3 copy.4
  246.0 1.5 fusion.9
  247.5 11.7 %cholesky.104 = f32[128,128]{1,0:T(8,128)S(1)} custom-call(f32[128,128]{1,0:T(8,128)S(1)} %cholesky.266), custom_call_target="Cholesky" | custom-call | tf_op jit(solution)/shard_map/jit(cholesky)/cholesky | solution.py:53
  259.2 0.1 cholesky.224
  259.4 9.8 %custom-call.30 = f32[1,128,128]{1,2,0:T(8,128)S(1)} custom-call(f32[1,128,128]{2,1,0:T(8,128)S(1)} %get-tuple-element.50), custom_call_target="InvertDiagBlocksLowerTriangular" | custom-call | tf_op jit(solution)/shard_map/jit(cholesky)/cholesky | solution.py:53
  269.2 0.3 constant_dynamic-update-slice_fusion.5
  269.5 0.3 convolution_subtract_fusion.6
  269.8 11.7 %cholesky.217 = f32[128,128]{1,0:T(8,128)S(1)} custom-call(f32[128,128]{1,0:T(8,128)S(1)} %cholesky.270), custom_call_target="Cholesky" | custom-call | tf_op jit(solution)/shard_map/jit(cholesky)/cholesky | solution.py:53
  281.6 0.6 compare_reduce_fusion.2
  282.2 0.6 compare_reduce_fusion.3
  282.9 9.9 %custom-call.31 = f32[1,128,128]{1,2,0:T(8,128)S(1)} custom-call(f32[1,128,128]{2,1,0:T(8,128)S(1)} %get-tuple-element.47), custom_call_target="InvertDiagBlocksLowerTriangular" | custom-call | tf_op jit(solution)/shard_map/jit(cholesky)/cholesky | solution.py:53
  292.8 0.3 convolution_dynamic-update-slice_fusion
  293.1 0.4 convolution_subtract_fusion.7
  293.5 11.7 %cholesky.238 = f32[128,128]{1,0:T(8,128)S(1)} custom-call(f32[128,128]{1,0:T(8,128)S(1)} %cholesky.275), custom_call_target="Cholesky" | custom-call | tf_op jit(solution)/shard_map/jit(cholesky)/cholesky | solution.py:53
  305.2 0.7 compare_reduce_fusion.1
  306.0 9.8 %custom-call.32 = f32[1,128,128]{1,2,0:T(8,128)S(1)} custom-call(f32[1,128,128]{2,1,0:T(8,128)S(1)} %get-tuple-element.44), custom_call_target="InvertDiagBlocksLowerTriangular" | custom-call | tf_op jit(solution)/shard_map/jit(cholesky)/cholesky | solution.py:53
  315.8 0.2 convolution_dynamic-update-slice_fusion.1
  316.0 0.4 convolution_subtract_fusion.8
  316.4 11.9 %cholesky.255 = f32[128,128]{1,0:T(8,128)S(1)} custom-call(f32[128,128]{1,0:T(8,128)S(1)} %convolution_subtract_fusion.8), custom_call_target="Cholesky" | custom-call | tf_op jit(solution)/shard_map/jit(cholesky)/cholesky | solution.py:53
  328.3 0.6 compare_reduce_fusion
  331.5 0.3 fusion.10
  331.8 8.0 %while.4 = (s32[]{:T(128)}, f32[512,512]{1,0:T(8,128)S(1)}, s32[4,2]{0,1:T(2,128)S(1)}, f32[4,128,128]{2,1,0:T(8,128)S(1)}, s32[]{:T(128)}) while((s32[]{:T(128)}, f32[512,512]{1,0:T(8,128)S(1)}, s32[4,2]{0,1:T(2,128)S(1)}, f32[4,128,128]{2,1,0:T(8,128)S(1)}, s32[]{:T(128)}) %tuple.41), condition=%wide.while_cond.clone, body=%wide.while_body.clone.sunk | while | flops 2 | bytes 131181 | solution.py:55
  331.8 0.1 constant_dynamic-slice_fusion.2
  331.9 0.5 fusion.75
  332.4 1.4 bitcast_dynamic-update-slice_fusion.2
  333.8 0.1 constant_dynamic-slice_fusion.2
  333.9 0.5 fusion.75
  334.4 1.4 bitcast_dynamic-update-slice_fusion.2
  335.8 0.1 constant_dynamic-slice_fusion.2
  335.9 0.5 fusion.75
  336.4 1.4 bitcast_dynamic-update-slice_fusion.2
  337.8 0.1 constant_dynamic-slice_fusion.2
  337.9 0.5 fusion.75
  338.4 1.4 bitcast_dynamic-update-slice_fusion.2
  339.8 39.3 %custom-call.35 = f32[4,128,128]{1,2,0:T(8,128)S(1)} custom-call(f32[4,128,128]{2,1,0:T(8,128)S(1)} %get-tuple-element.18), custom_call_target="InvertDiagBlocksLowerTriangular" | custom-call | tf_op jit(solution)/shard_map/jit(_solve_triangular)/triangular_solve | solution.py:55
  379.1 1.3 broadcast_multiply_fusion
  380.5 0.4 fusion.30
  380.9 0.6 convolution_subtract_fusion.3
  381.5 0.4 fusion.48
  381.9 1.0 convolution_subtract_fusion.2
  382.9 0.4 fusion.50
  383.4 1.5 convolution_subtract_fusion.5
  384.9 0.4 fusion.52
  385.4 0.4 fusion.28
  385.8 0.6 convolution_subtract_fusion.1
  386.4 0.4 fusion.47
  386.8 1.0 convolution_subtract_fusion
  387.9 0.4 fusion.49
  388.3 1.5 convolution_subtract_fusion.4
  389.8 0.4 fusion.51
  390.3 1.3 copy.7
  391.6 1.3 copy.6
  (17 shorter events, 0.4 us)
Async XLA Ops:
  7.2 184.0 %all-reduce.6.cloned.1.call-start = ((), (), s32[]{:S(2)}) async-start(), calls=%async_computation | async-start | bytes 4194304 | tf_op jit(solution)/shard_map/psum | solution.py:11
  8.7 39.3 %collective-permute-start = (f32[3073,128]{1,0:T(8,128)S(1)}, f32[3073,128]{1,0:T(8,128)S(1)}, u32[]{:S(2)}, u32[]{:S(2)}) collective-permute-start(f32[3073,128]{1,0:T(8,128)S(1)} %slice.124), channel_id=1, source_target_pairs={{1,0},{2,1},{3,2},{4,3},{5,4},{6,5},{7,6},{8,7},{9,8},{10,9},{11,1... | collective-permute-start | bytes 4720136 | tf_op jit(solution)/shard_map/ppermute | solution.py:18
  83.9 160.4 %all-reduce.8.cloned.1.call-start = ((), (), s32[]{:S(2)}) async-start(), calls=%async_computation.1 | async-start | bytes 4194304 | tf_op jit(solution)/shard_map/psum | solution.py:12
Sparse Core Ops, SparseCore 0:
  84.1 107.0 all-reduce.5
  193.6 50.6 all-reduce.7
